TPU v7x, 32 devices: a whole 2x2x4 slice. The times are simulated.
32 devices in a mesh: parts: 2 (over x), ctx: 16 (over z, y, core).
Axes of the slice: x: 2, y: 2, z: 4, core: 2. Of those that a mesh axis runs over, the one named last changes fastest.
Arguments:
- queries: bfloat16 [256, 8192], P(('parts', 'ctx')), parts along dimension 0, may hold values from -24 to 24
- steer_ids: int32 [256], P(('parts', 'ctx')), parts along dimension 0, may hold values from 0 to 15
- steer_table: bfloat16 [16, 8192], replicated, may hold values from -3 to 3
- kv: bfloat16 [2, 32768, 1024], P(None, ('parts', 'ctx')), parts along dimension 1, may hold values from -4 to 4
- blocks: int32 [4, 128], P('parts'), parts along dimension 0, may hold values from 0 to 255, as said below
- w_out: bfloat16 [8192, 8192], P('ctx'), may hold values from -0.0625 to 0.0625
Outputs:
- projected: bfloat16 [256, 8192], P(('parts', 'ctx')), parts along dimension 0
There are 2 independent parts, one for each index of `parts`. A program takes and returns all parts, laid end to end along the dimension named above; an argument that names none is the same for every part. Nothing has to cross between parts.
Inputs may be any that keep to these rules, and one draw needn't show every extreme that they name: Each row lists 128 distinct key blocks and always includes block 0 and block 255.
All inputs are finite; a program needn't handle non-finite values.
Results may differ from a plain program's by a relative error of at most 0.0066.
Values may be sent and summed in bfloat16 or wider, within the bound.
No kernel may reach another device: no remote copies, remote signals or barrier semaphores. Data moves between devices by JAX's collectives and lax.ppermute only.
A program may use at most 64 MiB of HBM per device.

v0:
```python
import jax
import jax.numpy as jnp
from jax import lax
from jax.sharding import PartitionSpec as P

HEADS = 64
KV_HEADS = 8
HEAD = 128
D = 8192
BLOCK = 64


def apply_steer(queries, steer_ids, steer_table):
    lookup_ids = jnp.arange(steer_table.shape[0], dtype=jnp.int32)
    one_hot = (steer_ids[:, None] == lookup_ids[None, :]).astype(jnp.bfloat16)
    lookup = jnp.dot(one_hot, steer_table, preferred_element_type=jnp.float32)
    return (queries.astype(jnp.float32) + lookup).astype(jnp.bfloat16)


def local_keep(blocks, first_block, block_count, query_count):
    block_ids = first_block + jnp.arange(block_count, dtype=jnp.int32)
    hits = jnp.any(blocks[:, :, None] == block_ids[None, None, :], axis=1)
    full = jnp.broadcast_to(
        hits[:, None, :, None], (query_count // BLOCK, BLOCK, block_count, BLOCK)
    )
    return full.reshape(query_count, block_count * BLOCK)


def group_attend(q_rows, k_rows, v_rows, keep_rows):
    scores = lax.dot_general(
        q_rows, k_rows, (((1,), (1,)), ((), ())), preferred_element_type=jnp.float32
    )
    scores = scores * HEAD ** (-0.5)
    masked = jnp.where(keep_rows, scores, jnp.float32(-1e30))
    row_peak = jnp.max(masked, axis=1)
    weights = jnp.where(keep_rows, jnp.exp(masked - row_peak[:, None]), jnp.float32(0.0))
    row_total = jnp.sum(weights, axis=1)
    probs = weights.astype(jnp.bfloat16)
    partial_out = jnp.dot(probs, v_rows, preferred_element_type=jnp.float32)
    return (row_peak, row_total, partial_out)


def partial_attention(steered, kv_piece, keep_mask):
    query_count = steered.shape[0]
    ctx_count = kv_piece.shape[1]
    group_size = HEADS // KV_HEADS
    q_groups = steered.reshape(query_count, KV_HEADS, group_size, HEAD).transpose(1, 2, 0, 3)
    q_groups = q_groups.reshape(KV_HEADS, group_size * query_count, HEAD)
    k_groups = kv_piece[0].reshape(ctx_count, KV_HEADS, HEAD).transpose(1, 0, 2)
    v_groups = kv_piece[1].reshape(ctx_count, KV_HEADS, HEAD).transpose(1, 0, 2)
    keep_rows = jnp.tile(keep_mask, (group_size, 1))

    def one_group(triple):
        return group_attend(triple[0], triple[1], triple[2], keep_rows)

    peaks, totals, outs = lax.map(one_group, (q_groups, k_groups, v_groups))
    peaks = (
        peaks.reshape(KV_HEADS, group_size, query_count)
        .transpose(2, 0, 1)
        .reshape(query_count, HEADS)
    )
    totals = (
        totals.reshape(KV_HEADS, group_size, query_count)
        .transpose(2, 0, 1)
        .reshape(query_count, HEADS)
    )
    outs = (
        outs.reshape(KV_HEADS, group_size, query_count, HEAD)
        .transpose(2, 0, 1, 3)
        .reshape(query_count, HEADS * HEAD)
    )
    return (peaks, totals, outs)


def per_device(queries, steer_ids, steer_table, kv, blocks, w_out):
    steered_local = apply_steer(queries, steer_ids, steer_table)
    steered = lax.all_gather(steered_local, "ctx", axis=0, tiled=True)
    shard_count = lax.axis_size("ctx")
    my_index = lax.axis_index("ctx")
    query_count = steered.shape[0]
    block_count = kv.shape[1] // BLOCK
    keep_mask = local_keep(blocks, my_index * block_count, block_count, query_count)
    peaks, totals, outs = partial_attention(steered, kv, keep_mask)
    stat_width = max(HEADS, shard_count)
    per_entry = D // stat_width
    col_count = D // shard_count

    def spread(values):
        return jnp.repeat(values, stat_width // HEADS, axis=1)

    got_num, got_max, got_den = (
        lax.all_to_all(outs, "ctx", split_axis=1, concat_axis=0, tiled=True),
        lax.all_to_all(spread(peaks), "ctx", split_axis=1, concat_axis=0, tiled=True),
        lax.all_to_all(spread(totals), "ctx", split_axis=1, concat_axis=0, tiled=True),
    )
    got_num = got_num.reshape(shard_count, query_count, col_count)
    got_max = got_max.reshape(shard_count, query_count, stat_width // shard_count)
    got_den = got_den.reshape(shard_count, query_count, stat_width // shard_count)
    overall = jnp.max(got_max, axis=0)
    scales = jnp.exp(got_max - overall[None])
    denominator = jnp.sum(scales * got_den, axis=0)
    numerator = jnp.sum(jnp.repeat(scales, per_entry, axis=2) * got_num, axis=0)
    attended = (numerator / jnp.repeat(denominator, per_entry, axis=1)).astype(jnp.bfloat16)
    return lax.psum_scatter(
        jnp.dot(attended, w_out, preferred_element_type=jnp.float32),
        "ctx",
        scatter_dimension=0,
        tiled=True,
    ).astype(jnp.bfloat16)


def solution(mesh):
    return jax.shard_map(
        per_device,
        mesh=mesh,
        in_specs=(
            P(("parts", "ctx"), None),
            P(("parts", "ctx")),
            P(),
            P(None, ("parts", "ctx"), None),
            P("parts", None),
            P("ctx", None),
        ),
        out_specs=P(("parts", "ctx"), None),
        check_vma=False,
    )
```

profile of v0, /device:TPU:0, one launch (start us, length us, event | category | flops | bytes accessed | tf_op | source)
XLA Modules:
  0.0 324.4 jit_solution(4779056116548888666)
XLA Ops:
  6.5 0.9 copy-done
  7.5 1.8 fusion.25
  9.3 4.0 %fusion.32 = (bf16[1,1024,1024]{2,1,0:T(8,128)(2,1)S(1)}, bf16[1,1024,1024]{2,1,0:T(8,128)(2,1)}) fusion(bf16[2,1024,1024]{2,1,0:T(8,128)(2,1)} %param.11), kind=kLoop, calls=%fused_computation.38 | loop fusion | bytes 8388608 | tf_op jit(solution)/shard_map/slice | solution.py:50
  13.4 4.0 %copy.38 = bf16[1,1024,1024]{1,2,0:T(8,128)(2,1)} copy(bf16[1,1024,1024]{2,1,0:T(8,128)(2,1)} %get-tuple-element.124) | data formatting | bytes 4194304
  17.3 2.6 copy.39
  19.9 0.2 compare_reduce_fusion
  20.1 0.1 broadcast_in_dim.42
  20.2 0.4 tile.10
  20.6 0.3 copy.34
  20.9 32.8 %all-gather.2.cloned.1.call-done = bf16[128,8192]{1,0:T(8,128)(2,1)} async-done(((bf16[8,8192]{1,0:T(8,128)(2,1)}), bf16[128,8192]{1,0:T(8,128)(2,1)}) %all-gather.2.cloned.1.call-update) | async-done | bytes 2097168 | tf_op jit(solution)/shard_map/all_gather | solution.py:77
  53.7 2.2 copy.41
  55.9 1.4 copy.29
  57.3 58.5 %while.15 = (s32[]{:T(128)}, f32[8,1024]{1,0:T(8,128)S(1)}, f32[8,1024]{1,0:T(8,128)S(1)}, f32[8,1024,128]{2,1,0:T(8,128)}, bf16[8,1024,128]{2,1,0:T(8,128)(2,1)...) while((s32[]{:T(128)}, f32[8,1024]{1,0:T(8,128)S(1)}, ...), condition=%wide.region_4.5_spmd.clone, body=%wide.region_1.4_spmd.clone.sunk | while | flops 550500352 | bytes 18253932 | solution.py:56
  57.3 0.5 tile.22
  57.8 2.0 fusion.44
  59.8 3.2 fusion.46
  63.0 1.3 fusion.45
  64.3 0.1 dynamic_update_slice.20
  64.4 0.1 dynamic_update_slice.19
  64.6 0.5 tile.22
  65.1 2.0 fusion.44
  67.1 3.2 fusion.46
  70.3 1.3 fusion.45
  71.6 0.1 dynamic_update_slice.20
  71.8 0.1 dynamic_update_slice.19
  71.9 0.5 tile.22
  72.4 2.0 fusion.44
  74.4 3.2 fusion.46
  77.7 1.3 fusion.45
  79.0 0.1 dynamic_update_slice.20
  79.1 0.1 dynamic_update_slice.19
  79.2 0.5 tile.22
  79.7 2.0 fusion.44
  81.7 3.2 fusion.46
  85.0 1.3 fusion.45
  86.5 0.5 tile.22
  87.0 2.0 fusion.44
  89.1 3.2 fusion.46
  92.3 1.3 fusion.45
  93.8 0.5 tile.22
  94.3 2.0 fusion.44
  96.4 3.2 fusion.46
  99.6 1.3 fusion.45
  101.2 0.5 tile.22
  101.6 2.0 fusion.44
  103.7 3.2 fusion.46
  106.9 1.3 fusion.45
  108.4 0.5 tile.22
  108.9 2.0 fusion.44
  111.0 3.2 fusion.46
  114.2 1.3 fusion.45
  115.8 0.6 copy.58
  116.4 3.5 %all-to-all-start = ((f32[128,16,4]{0,2,1:T(4,128)}), f32[128,16,4]{0,2,1:T(4,128)S(1)}, u32[]{:S(2)}, u32[]{:S(2)}) async-start(f32[128,16,4]{0,2,1:T(4,128)} %bitcast.7), calls=%async_computation | async-start | bytes 65536 | tf_op jit(solution)/shard_map/all_to_all | solution.py:93
  119.9 0.6 copy.57
  120.5 6.0 %all-to-all-done = f32[128,16,4]{0,2,1:T(4,128)S(1)} async-done(((f32[128,16,4]{0,2,1:T(4,128)}), f32[128,16,4]{0,2,1:T(4,128)S(1)}, u32[]{:S(2)}, u32[]{:S(2)}) %all-to-all-start) | async-done | bytes 32800 | tf_op jit(solution)/shard_map/all_to_all | solution.py:93
  126.5 3.5 %all-to-all-start.2 = ((f32[128,16,4]{0,2,1:T(4,128)}), f32[128,16,4]{0,2,1:T(4,128)S(1)}, u32[]{:S(2)}, u32[]{:S(2)}) async-start(f32[128,16,4]{0,2,1:T(4,128)} %bitcast.15), calls=%async_computation.2 | async-start | bytes 65536 | tf_op jit(solution)/shard_map/all_to_all | solution.py:94
  130.0 5.4 %copy.35 = f32[128,8,8,128]{0,3,2,1:T(8,128)} copy(f32[128,8,8,128]{3,0,2,1:T(8,128)} %bitcast.11) | data formatting | bytes 8388608 | tf_op jit(solution)/shard_map/transpose | solution.py:69
  135.3 1.2 all-to-all-done.2
  136.6 4.8 %all-to-all-start.1 = ((f32[128,16,512]{0,2,1:T(8,128)}), f32[128,16,512]{0,2,1:T(8,128)}, u32[]{:S(2)}, u32[]{:S(2)}) async-start(f32[128,16,512]{0,2,1:T(8,128)} %bitcast.118), calls=%async_computation.1 | async-start | bytes 8388608 | tf_op jit(solution)/shard_map/all_to_all | solution.py:92
  141.5 77.4 %all-to-all-done.1 = f32[128,16,512]{0,2,1:T(8,128)} async-done(((f32[128,16,512]{0,2,1:T(8,128)}), f32[128,16,512]{0,2,1:T(8,128)}, u32[]{:S(2)}, u32[]{:S(2)}) %all-to-all-start.1) | async-done | bytes 4194336 | tf_op jit(solution)/shard_map/all_to_all | solution.py:92
  218.9 2.5 fusion.26
  221.4 6.6 %fusion.33 = f32[128,8192]{1,0:T(8,128)} fusion(bf16[128,512]{0,1:T(8,128)(2,1)S(1)} %fusion.27, bf16[512,8192]{1,0:T(8,128)(2,1)} %param.13), kind=kOutput, calls=%fused_computation.39 | convolution fusion | flops 1073741824 | bytes 12713984 | tf_op jit(solution)/shard_map/dot_general | solution.py:105
  228.1 87.8 %reduce-scatter.2.cloned.1.call-done = f32[8,8192]{1,0:T(8,128)} async-done(((f32[128,8192]{1,0:T(8,128)}), f32[8,8192]{1,0:T(8,128)}) %reduce-scatter.2.cloned.1.call-update) | async-done | bytes 262160 | tf_op jit(solution)/shard_map/reduce_scatter | solution.py:104
  315.9 1.6 convert_element_type.19
  (24 shorter events, 1.3 us)
Async XLA Ops:
  6.5 1.0 copy-start
  6.5 47.2 %all-gather.2.cloned.1.call-start = ((), (), s32[]{:S(2)}) async-start(), calls=%async_computation.4 | async-start | bytes 2228224 | tf_op jit(solution)/shard_map/all_gather | solution.py:77
  13.4 6.5 %copy-start.1 = (s32[2,128]{1,0:T(2,128)S(1)}, s32[2,128]{1,0:T(2,128)}, u32[]{:S(2)}) copy-start(s32[2,128]{1,0:T(2,128)} %param.12) | copy-start | bytes 3076
  116.4 10.1 %all-to-all-start = ((f32[128,16,4]{0,2,1:T(4,128)}), f32[128,16,4]{0,2,1:T(4,128)S(1)}, u32[]{:S(2)}, u32[]{:S(2)}) async-start(f32[128,16,4]{0,2,1:T(4,128)} %bitcast.7), calls=%async_computation | async-start | bytes 65536 | tf_op jit(solution)/shard_map/all_to_all | solution.py:93
  126.5 10.1 %all-to-all-start.2 = ((f32[128,16,4]{0,2,1:T(4,128)}), f32[128,16,4]{0,2,1:T(4,128)S(1)}, u32[]{:S(2)}, u32[]{:S(2)}) async-start(f32[128,16,4]{0,2,1:T(4,128)} %bitcast.15), calls=%async_computation.2 | async-start | bytes 65536 | tf_op jit(solution)/shard_map/all_to_all | solution.py:94
  136.6 82.3 %all-to-all-start.1 = ((f32[128,16,512]{0,2,1:T(8,128)}), f32[128,16,512]{0,2,1:T(8,128)}, u32[]{:S(2)}, u32[]{:S(2)}) async-start(f32[128,16,512]{0,2,1:T(8,128)} %bitcast.118), calls=%async_computation.1 | async-start | bytes 8388608 | tf_op jit(solution)/shard_map/all_to_all | solution.py:92
  141.3 174.6 %reduce-scatter.2.cloned.1.call-start = ((), (), s32[]{:S(2)}) async-start(), calls=%async_computation.5 | async-start | bytes 4456448 | tf_op jit(solution)/shard_map/reduce_scatter | solution.py:104
Sparse Core Ops, SparseCore 0:
  9.5 44.1 all-gather.1
  228.2 87.6 reduce-scatter.1
where the time goes:
time: 326 us; the launch traced here: 324 us
  waiting for transfers between devices  205 us (63%)
  matrix products  50.6 us (16%)
  local copies, waits for them, and re-layouts  28 us (9%)
  other arithmetic  14.8 us (5%)
  between operations  13.5 us (4%)
  starting transfers between devices  11.8 us (4%)
    reduce_scatter x1, waiting for transfers between devices, per_device(): lax.psum_scatter(jnp.dot(attended, w_out, preferred_element_type=jnp.floa...  87.8 us
    all_to_all x1, waiting for transfers between devices, per_device(): lax.all_to_all(outs, 'ctx', split_axis=1, concat_axis=0, tiled=True)  77.4 us
    all_gather x1, waiting for transfers between devices, per_device(): steered = lax.all_gather(steered_local, 'ctx', axis=0, tiled=True)  32.8 us
    dot_general x8, matrix products, group_attend(): partial_out = jnp.dot(probs, v_rows, preferred_element_type=jnp.float32)  25.8 us
    dot_general x8, matrix products, group_attend(): lax.dot_general(q_rows, k_rows, (((1,), (1,)), ((), ())), preferred_eleme...  16.4 us
    unnamed x10, local copies, waits for them, and re-layouts  11.2 us
    reduce_sum x8, other arithmetic, group_attend(): row_total = jnp.sum(weights, axis=1)  10.4 us
    dot_general x1, matrix products, per_device(): jnp.dot(attended, w_out, preferred_element_type=jnp.float32)  6.63 us
  transfers between devices with their start and end apart: 5, of which 5 were waited for; matrix products, arithmetic and copies ran while one was open for 5% of the time, Pallas kernels for 0%

commit v1 on v0

--- a/solution.py
+++ b/solution.py
@@ -8,6 +8,12 @@
 HEAD = 128
 D = 8192
 BLOCK = 64
+
+
+def swap_blocks(x, mesh_axis, split, join):
+    pieces = jnp.split(x, lax.axis_size(mesh_axis), axis=split)
+    got = lax.all_to_all(jnp.stack(pieces), mesh_axis, 0, 0)
+    return jnp.concatenate(got, axis=join)
 
 
 def apply_steer(queries, steer_ids, steer_table):
@@ -89,7 +95,7 @@
         return jnp.repeat(values, stat_width // HEADS, axis=1)
 
     got_num, got_max, got_den = (
-        lax.all_to_all(outs, "ctx", split_axis=1, concat_axis=0, tiled=True),
+        swap_blocks(outs, "ctx", 1, 0),
         lax.all_to_all(spread(peaks), "ctx", split_axis=1, concat_axis=0, tiled=True),
         lax.all_to_all(spread(totals), "ctx", split_axis=1, concat_axis=0, tiled=True),
     )

time: 326 us -> 355 us (1.089)
  local copies, waits for them, and re-layouts: 28 us -> 54.7 us
    unnamed x10 -> x25, local copies, waits for them, and re-layouts: 11.2 us -> 36.3 us
    all_to_all x1, waiting for transfers between devices: 1.24 us -> 4.91 us  [per_device(): lax.all_to_all(spread(totals), 'ctx', split_axis=1, concat_axis=0, tiled=...]
  transfers between devices with their start and end apart: 5 -> 5, of which waited for: 5 -> 5; matrix products, arithmetic and copies ran while one was open for 5% -> 4% of each run, Pallas kernels for 0% -> 0%
where the time goes in v1:
time: 355 us; the launch traced here: 353 us
  waiting for transfers between devices  207 us (58%)
  local copies, waits for them, and re-layouts  54.7 us (15%)
  matrix products  50.6 us (14%)
  other arithmetic  14.8 us (4%)
  between operations  13.5 us (4%)
  starting transfers between devices  11.6 us (3%)
    reduce_scatter x1, waiting for transfers between devices, per_device(): lax.psum_scatter(jnp.dot(attended, w_out, preferred_element_type=jnp.floa...  87.9 us
    all_to_all x1, waiting for transfers between devices, swap_blocks(): got = lax.all_to_all(jnp.stack(pieces), mesh_axis, 0, 0)  77.4 us
    unnamed x25, local copies, waits for them, and re-layouts  36.3 us
    all_gather x1, waiting for transfers between devices, per_device(): steered = lax.all_gather(steered_local, 'ctx', axis=0, tiled=True)  32.8 us
    dot_general x8, matrix products, group_attend(): partial_out = jnp.dot(probs, v_rows, preferred_element_type=jnp.float32)  25.8 us
    dot_general x8, matrix products, group_attend(): lax.dot_general(q_rows, k_rows, (((1,), (1,)), ((), ())), preferred_eleme...  16.4 us
    reduce_sum x8, other arithmetic, group_attend(): row_total = jnp.sum(weights, axis=1)  10.4 us
  transfers between devices with their start and end apart: 5, of which 5 were waited for; matrix products, arithmetic and copies ran while one was open for 4% of the time, Pallas kernels for 0%

profile of v1, /device:TPU:0, one launch (start us, length us, event | category | flops | bytes accessed | tf_op | source)
XLA Modules:
  0.0 352.9 jit_solution(2199296953665771616)
XLA Ops:
  6.5 0.9 copy-done
  7.5 1.8 fusion.25
  9.3 4.0 %fusion.48 = (bf16[1,1024,1024]{2,1,0:T(8,128)(2,1)S(1)}, bf16[1,1024,1024]{2,1,0:T(8,128)(2,1)}) fusion(bf16[2,1024,1024]{2,1,0:T(8,128)(2,1)} %param.11), kind=kLoop, calls=%fused_computation.70 | loop fusion | bytes 8388608 | tf_op jit(solution)/shard_map/slice | solution.py:56
  13.3 4.0 %copy.38 = bf16[1,1024,1024]{1,2,0:T(8,128)(2,1)} copy(bf16[1,1024,1024]{2,1,0:T(8,128)(2,1)} %get-tuple-element.124) | data formatting | bytes 4194304
  17.3 2.6 copy.39
  20.9 32.8 %all-gather.2.cloned.1.call-done = bf16[128,8192]{1,0:T(8,128)(2,1)} async-done(((bf16[8,8192]{1,0:T(8,128)(2,1)}), bf16[128,8192]{1,0:T(8,128)(2,1)}) %all-gather.2.cloned.1.call-update) | async-done | bytes 2097168 | tf_op jit(solution)/shard_map/all_gather | solution.py:83
  53.7 2.2 copy.41
  55.9 1.4 copy.29
  57.3 58.5 %while.15 = (s32[]{:T(128)}, f32[8,1024]{1,0:T(8,128)S(1)}, f32[8,1024]{1,0:T(8,128)S(1)}, f32[8,1024,128]{2,1,0:T(8,128)}, bf16[8,1024,128]{2,1,0:T(8,128)(2,1)...) while((s32[]{:T(128)}, f32[8,1024]{1,0:T(8,128)S(1)}, ...), condition=%wide.region_4.5_spmd.clone, body=%wide.region_1.4_spmd.clone.sunk | while | flops 550500352 | bytes 18253932 | solution.py:62
  57.3 0.5 tile.22
  57.8 2.0 fusion.60
  59.8 3.2 fusion.62
  63.0 1.3 fusion.61
  64.6 0.5 tile.22
  65.1 2.0 fusion.60
  67.1 3.2 fusion.62
  70.4 1.3 fusion.61
  72.4 2.0 fusion.60
  74.4 3.2 fusion.62
  77.7 1.3 fusion.61
  79.7 2.0 fusion.60
  81.8 3.2 fusion.62
  85.0 1.3 fusion.61
  87.0 2.0 fusion.60
  89.1 3.2 fusion.62
  92.3 1.3 fusion.61
  94.3 2.0 fusion.60
  96.4 3.2 fusion.62
  99.6 1.3 fusion.61
  101.7 2.0 fusion.60
  103.7 3.2 fusion.62
  106.9 1.3 fusion.61
  109.0 2.0 fusion.60
  111.0 3.2 fusion.62
  114.2 1.3 fusion.61
  115.8 5.4 %copy.35 = f32[128,8,8,128]{0,3,2,1:T(8,128)} copy(f32[128,8,8,128]{3,0,2,1:T(8,128)} %bitcast.11) | data formatting | bytes 8388608 | tf_op jit(solution)/shard_map/transpose | solution.py:75
  121.1 1.7 fusion.42
  122.8 1.7 fusion.41
  124.5 1.7 fusion.40
  126.1 1.7 fusion.39
  127.8 1.7 fusion.38
  129.5 1.7 fusion.37
  131.2 1.7 fusion.36
  132.9 1.7 fusion.35
  134.5 1.7 fusion.34
  136.2 1.7 fusion.33
  137.9 1.7 fusion.32
  139.6 1.7 fusion.31
  141.2 1.7 fusion.30
  142.9 1.7 fusion.29
  144.6 0.6 copy.58
  145.2 3.5 all-to-all-start
  148.7 1.7 fusion.28
  150.3 0.6 copy.57
  150.9 4.3 %all-to-all-done = f32[128,16,4]{0,2,1:T(4,128)S(1)} async-done(((f32[128,16,4]{0,2,1:T(4,128)}), f32[128,16,4]{0,2,1:T(4,128)S(1)}, u32[]{:S(2)}, u32[]{:S(2)}) %all-to-all-start) | async-done | bytes 32800 | tf_op jit(solution)/shard_map/all_to_all | solution.py:99
  155.2 3.5 all-to-all-start.2
  158.8 1.7 fusion.27
  160.4 4.9 %all-to-all-done.2 = f32[128,16,4]{0,2,1:T(4,128)S(1)} async-done(((f32[128,16,4]{0,2,1:T(4,128)}), f32[128,16,4]{0,2,1:T(4,128)S(1)}, u32[]{:S(2)}, u32[]{:S(2)}) %all-to-all-start.2) | async-done | bytes 32800 | tf_op jit(solution)/shard_map/all_to_all | solution.py:100
  165.4 4.5 %all-to-all-start.1 = ((f32[16,128,512]{1,2,0:T(8,128)}), f32[16,128,512]{1,2,0:T(8,128)}, u32[]{:S(2)}, u32[]{:S(2)}) async-start(f32[16,128,512]{1,2,0:T(8,128)} %fusion.27), calls=%async_computation.1 | async-start | bytes 8388608 | tf_op jit(solution)/shard_map/all_to_all | solution.py:15
  170.0 77.4 %all-to-all-done.1 = f32[16,128,512]{1,2,0:T(8,128)} async-done(((f32[16,128,512]{1,2,0:T(8,128)}), f32[16,128,512]{1,2,0:T(8,128)}, u32[]{:S(2)}, u32[]{:S(2)}) %all-to-all-start.1) | async-done | bytes 4194336 | tf_op jit(solution)/shard_map/all_to_all | solution.py:15
  247.4 2.5 fusion.26
  249.9 6.6 %fusion.49 = f32[128,8192]{1,0:T(8,128)} fusion(bf16[128,512]{0,1:T(8,128)(2,1)S(1)} %fusion.43, bf16[512,8192]{1,0:T(8,128)(2,1)} %param.13), kind=kOutput, calls=%fused_computation.71 | convolution fusion | flops 1073741824 | bytes 12713984 | tf_op jit(solution)/shard_map/dot_general | solution.py:111
  256.6 87.9 %reduce-scatter.2.cloned.1.call-done = f32[8,8192]{1,0:T(8,128)} async-done(((f32[128,8192]{1,0:T(8,128)}), f32[8,8192]{1,0:T(8,128)}) %reduce-scatter.2.cloned.1.call-update) | async-done | bytes 262160 | tf_op jit(solution)/shard_map/reduce_scatter | solution.py:110
  344.5 1.6 convert_element_type.19
  (40 shorter events, 5.8 us)
Async XLA Ops:
  6.5 1.0 copy-start
  6.5 47.2 %all-gather.2.cloned.1.call-start = ((), (), s32[]{:S(2)}) async-start(), calls=%async_computation.4 | async-start | bytes 2228224 | tf_op jit(solution)/shard_map/all_gather | solution.py:83
  13.3 6.6 %copy-start.1 = (s32[2,128]{1,0:T(2,128)S(1)}, s32[2,128]{1,0:T(2,128)}, u32[]{:S(2)}) copy-start(s32[2,128]{1,0:T(2,128)} %param.12) | copy-start | bytes 3076
  145.2 10.1 %all-to-all-start = ((f32[128,16,4]{0,2,1:T(4,128)}), f32[128,16,4]{0,2,1:T(4,128)S(1)}, u32[]{:S(2)}, u32[]{:S(2)}) async-start(f32[128,16,4]{0,2,1:T(4,128)} %bitcast.7), calls=%async_computation | async-start | bytes 65536 | tf_op jit(solution)/shard_map/all_to_all | solution.py:99
  155.2 10.1 %all-to-all-start.2 = ((f32[128,16,4]{0,2,1:T(4,128)}), f32[128,16,4]{0,2,1:T(4,128)S(1)}, u32[]{:S(2)}, u32[]{:S(2)}) async-start(f32[128,16,4]{0,2,1:T(4,128)} %bitcast.30), calls=%async_computation.2 | async-start | bytes 65536 | tf_op jit(solution)/shard_map/all_to_all | solution.py:100
  165.4 82.0 %all-to-all-start.1 = ((f32[16,128,512]{1,2,0:T(8,128)}), f32[16,128,512]{1,2,0:T(8,128)}, u32[]{:S(2)}, u32[]{:S(2)}) async-start(f32[16,128,512]{1,2,0:T(8,128)} %fusion.27), calls=%async_computation.1 | async-start | bytes 8388608 | tf_op jit(solution)/shard_map/all_to_all | solution.py:15
  169.9 174.6 %reduce-scatter.2.cloned.1.call-start = ((), (), s32[]{:S(2)}) async-start(), calls=%async_computation.5 | async-start | bytes 4456448 | tf_op jit(solution)/shard_map/reduce_scatter | solution.py:110
Sparse Core Ops, SparseCore 0:
  9.5 44.1 all-gather.1
  256.7 87.7 reduce-scatter.1
